TPU v7x, 256 devices: a whole 4x4x8 slice. The times are simulated.
256 devices in a mesh: dp: 2 (over core), ctx: 16 (over z_hi, y), exp: 8 (over x, z_lo).
Axes of the slice: x: 4, y: 4, z: 8 (z_hi: 4, z_lo: 2; z = z_hi * 2 + z_lo), core: 2. Of those that a mesh axis runs over, the one named last changes fastest.
Arguments:
- tokens: bfloat16 [2, 2048, 2560], P('dp', 'ctx'), may hold values from -6 to 6
- queries: bfloat16 [2, 2048, 16, 576], P('dp', 'ctx', 'exp'), may hold values from -240 to 240
- kv_weight: bfloat16 [2560, 576], P('exp'), may hold values from -0.125 to 0.125
- kv_gain: bfloat16 [512], replicated, may hold values from 0.5 to 1.5
- uv_weight: bfloat16 [16, 512, 128], P('exp'), may hold values from -0.75 to 0.75
- out_weight: bfloat16 [2048, 2560], P('exp'), may hold values from -0.5 to 0.5
- post_gain: bfloat16 [2560], replicated, may hold values from 0.5 to 1.5
- router_weight: bfloat16 [2560, 32], replicated, may hold values from -0.125 to 0.125
- expert_ids: int32 [2, 2048, 6], P('dp', 'ctx'), may hold values from 0 to 31, all different within a row; in each aligned block of 128 rows (0 to 127, 128 to 255, ..., all dimensions but the last counted through in order) at most 32 rows name the same one
- doc_ids: int32 [2, 2048], P('dp', 'ctx'), may hold values from 0 to 3, never falling along the last dimension, each value on 1 to 1024 neighbouring positions
- gate_weight: bfloat16 [32, 2560, 1536], P('ctx', None, 'exp'), may hold values from -0.125 to 0.125
- up_weight: bfloat16 [32, 2560, 1536], P('ctx', None, 'exp'), may hold values from -0.125 to 0.125
- down_weight: bfloat16 [32, 1536, 2560], P('ctx', 'exp'), may hold values from -0.15625 to 0.15625
- cotangent: bfloat16 [2, 2048, 2560], P('dp', 'ctx'), may hold values from -6 to 6
Outputs:
- layer_out: bfloat16 [2, 2048, 2560], P('dp', 'ctx')
- router_grad: float32 [2560, 32], replicated
- gate_grad: bfloat16 [32, 2560, 1536], P('ctx', 'dp', 'exp')
- up_grad: bfloat16 [32, 2560, 1536], P('ctx', 'dp', 'exp')
- down_grad: bfloat16 [32, 1536, 2560], P('ctx', 'exp', 'dp')
Inputs may be any that keep to these rules, and one draw needn't show every extreme that they name: `expert_ids`: in each aligned block of 128 positions of a sequence no expert is named by more than 32 of the block's assignments; the experts of one token differ. `doc_ids`: document numbers never fall along a sequence; a document has at most 1024 positions.
All inputs are finite; a program needn't handle non-finite values.
Results may differ from a plain program's by a relative error of at most 0.023.
The roundings to bfloat16 on the way count: a program that leaves them out, or rounds other values in their place, can miss the bound.
Values may be sent and summed in bfloat16 or wider, within the bound.
No kernel may reach another device: no remote copies, remote signals or barrier semaphores. Data moves between devices by JAX's collectives and lax.ppermute only.
A program may use at most 128 MiB of HBM per device.

v0:
```python
import jax
import jax.numpy as jnp
from jax import lax
from jax.sharding import PartitionSpec as P

ROPE = 64
NOPE = 128
epsilon = 1e-06


def from_everyone(array, axis):
    count = lax.axis_size(axis)
    return lax.all_to_all(
        jnp.broadcast_to(array[None], (count, *array.shape)), axis, 0, 0, tiled=True
    )


def taken_together(array, axis):
    everything = from_everyone(array, axis)
    return jnp.sum(everything, axis=0)


def in_one_piece(arrays, axis, split_dim, concat_dim, along):
    both = jnp.concatenate(arrays, axis=along)
    result, at, gathered = (
        lax.all_to_all(both, axis, split_axis=split_dim, concat_axis=concat_dim, tiled=True),
        0,
        [],
    )
    for a in arrays:
        gathered.append(lax.slice_in_dim(result, at, at + a.shape[along], axis=along))
        at += a.shape[along]
    return tuple(gathered)


def rms_scale(values, gain):
    return values * lax.rsqrt(jnp.mean(values * values, axis=-1, keepdims=True) + epsilon) * gain


def rotate(rope_part, positions):
    half_width = rope_part.shape[-1] // 2
    frequency = jnp.power(
        10000.0, -2.0 * jnp.arange(half_width, dtype=jnp.float32) / rope_part.shape[-1]
    )
    angles = positions.astype(jnp.float32)[:, None] * frequency[None, :]
    cosine = jnp.cos(angles)
    sine_part = jnp.sin(angles)
    first_half = rope_part[:, :half_width]
    second = rope_part[:, half_width:]
    return jnp.concatenate(
        [first_half * cosine - second * sine_part, second * cosine + first_half * sine_part], axis=1
    )


def route_slots(outgoing):
    moved = lax.all_to_all(outgoing, ("dp", "ctx"), split_axis=0, concat_axis=0, tiled=True)
    return moved


def local(
    tokens,
    queries,
    kv_weight,
    kv_gain,
    uv_weight,
    out_weight,
    post_gain,
    router_weight,
    expert_ids,
    doc_ids,
    gate_weight,
    up_weight,
    down_weight,
    cotangent,
):
    local_rows = tokens[0]
    seq_rows = local_rows.shape[0]
    model_width = local_rows.shape[1]
    latent_width = kv_gain.shape[0]
    row_share = kv_weight.shape[0]
    columns = lax.dynamic_slice_in_dim(local_rows, lax.axis_index("exp") * row_share, row_share, 1)
    compressed = taken_together(
        jnp.dot(columns, kv_weight, preferred_element_type=jnp.float32), "exp"
    )
    positions = lax.axis_index("ctx") * seq_rows + jnp.arange(seq_rows, dtype=jnp.int32)
    latent = rms_scale(compressed[:, :latent_width], kv_gain.astype(jnp.float32)).astype(
        jnp.bfloat16
    )
    rope_key = rotate(compressed[:, latent_width:], positions).astype(jnp.bfloat16)
    key_rows = jnp.concatenate([latent, rope_key], axis=1)
    all_keys, all_docs = (
        lax.all_gather(key_rows, "ctx", axis=0, tiled=True),
        lax.all_gather(doc_ids[0], "ctx", axis=0, tiled=True),
    )
    key_positions = jnp.arange(all_keys.shape[0], dtype=jnp.int32)
    allowed = (key_positions[None, :] <= positions[:, None]) & (
        all_docs[None, :] == doc_ids[0][:, None]
    )
    allowed = allowed[:, None, :]
    score_scale = (NOPE + ROPE) ** (-0.5)
    scores = (
        jnp.einsum("qhd,kd->qhk", queries[0], all_keys, preferred_element_type=jnp.float32)
        * score_scale
    )
    score_peak = jnp.max(jnp.where(allowed, scores, -1e30), axis=-1, keepdims=True)
    weights = jnp.exp(jnp.where(allowed, scores - score_peak, -1e30))
    weight_total = jnp.sum(weights, axis=-1, keepdims=True)
    mixed_latent = (
        jnp.einsum(
            "qhk,kl->qhl",
            weights.astype(jnp.bfloat16),
            all_keys[:, :latent_width],
            preferred_element_type=jnp.float32,
        )
        / weight_total
    )
    mixed_latent = mixed_latent.astype(jnp.bfloat16)
    head_values = (
        jnp.einsum("qhl,hlv->qhv", mixed_latent, uv_weight, preferred_element_type=jnp.float32)
        .astype(jnp.bfloat16)
        .reshape(seq_rows, -1)
    )
    head_part = jnp.dot(head_values, out_weight, preferred_element_type=jnp.float32)
    attention = lax.psum(head_part, "exp")
    hidden = (local_rows.astype(jnp.float32) + attention).astype(jnp.bfloat16)
    normed = rms_scale(hidden.astype(jnp.float32), post_gain.astype(jnp.float32)).astype(
        jnp.bfloat16
    )
    logits = jnp.dot(normed, router_weight, preferred_element_type=jnp.float32)
    router_probs = jax.nn.softmax(logits, axis=-1)
    picked_ids = expert_ids[0]
    experts_all = router_weight.shape[1]
    top_count = picked_ids.shape[1]
    chosen = jnp.take_along_axis(router_probs, picked_ids, axis=1)
    chosen_sum = jnp.sum(chosen, axis=1, keepdims=True)
    route_w = chosen / chosen_sum
    route_wb = route_w.astype(jnp.bfloat16)
    ctx_count = lax.axis_size("ctx")
    held_experts = experts_all // ctx_count
    capacity = (4 * seq_rows * top_count + 3 * experts_all - 1) // (3 * experts_all)
    flat_ids = picked_ids.reshape(-1)
    onehot = (flat_ids[:, None] == jnp.arange(experts_all, dtype=jnp.int32)[None, :]).astype(
        jnp.int32
    )
    slot_rank = jnp.sum((jnp.cumsum(onehot, axis=0) - onehot) * onehot, axis=1).reshape(
        seq_rows, top_count
    )
    dp_count = lax.axis_size("dp")
    local_count = held_experts // dp_count
    first_local = lax.axis_index("dp") * local_count
    gate_local = lax.dynamic_slice_in_dim(gate_weight, first_local, local_count, 0)
    up_local = lax.dynamic_slice_in_dim(up_weight, first_local, local_count, 0)
    down_local = lax.dynamic_slice_in_dim(down_weight, first_local, local_count, 0)
    home_ctx = picked_ids // held_experts
    remainder = picked_ids % held_experts
    home_dp = remainder // local_count
    within = remainder % local_count
    slot_index = ((home_dp * ctx_count + home_ctx) * local_count + within) * capacity + slot_rank
    slot_hits = (
        slot_index[:, :, None] == jnp.arange(experts_all * capacity, dtype=jnp.int32)[None, None, :]
    )
    dispatch = jnp.any(slot_hits, axis=1).astype(jnp.bfloat16)
    combine = jnp.sum(
        jnp.where(slot_hits, route_wb[:, :, None], jnp.zeros((), jnp.bfloat16)), axis=1
    )
    outgoing = jnp.einsum("se,sd->ed", dispatch, normed, preferred_element_type=jnp.float32).astype(
        jnp.bfloat16
    )
    outgoing = outgoing.reshape(-1, local_count, capacity, model_width)
    arrived = route_slots(outgoing)
    gate_pre = jnp.einsum("sjcd,jdf->sjcf", arrived, gate_local, preferred_element_type=jnp.float32)
    up_pre = jnp.einsum("sjcd,jdf->sjcf", arrived, up_local, preferred_element_type=jnp.float32)
    activated = (jax.nn.silu(gate_pre) * up_pre).astype(jnp.bfloat16)
    expert_part = jnp.einsum(
        "sjcf,jfd->sjcd", activated, down_local, preferred_element_type=jnp.float32
    ).astype(jnp.bfloat16)
    returned = lax.all_to_all(expert_part, ("dp", "ctx"), split_axis=0, concat_axis=0, tiled=True)
    returned = returned.reshape(experts_all * capacity, model_width)
    moe_part = jnp.dot(combine, returned, preferred_element_type=jnp.float32)
    cot_rows = cotangent[0]
    cross_terms = jnp.einsum("sd,ed->se", cot_rows, returned, preferred_element_type=jnp.float32)
    dweight_part = jnp.take_along_axis(cross_terms, slot_index, axis=1)
    moe, dweight = lax.psum((moe_part, dweight_part), "exp")
    layer_out = (hidden.astype(jnp.float32) + moe).astype(jnp.bfloat16)
    mean_term = jnp.sum(dweight * route_w, axis=1, keepdims=True)
    dchosen = (dweight - mean_term) / chosen_sum
    id_hits = (
        picked_ids[:, :, None] == jnp.arange(experts_all, dtype=jnp.int32)[None, None, :]
    ).astype(jnp.float32)
    dprobs = jnp.sum(id_hits * dchosen[:, :, None], axis=1)
    dlogits = router_probs * (dprobs - jnp.sum(router_probs * dprobs, axis=1, keepdims=True))
    router_term = jnp.dot(normed.astype(jnp.float32).T, dlogits, precision=lax.Precision.HIGHEST)
    router_grad = lax.psum(router_term, ("dp", "ctx"))
    slot_cot = jnp.einsum(
        "se,sd->ed", combine, cot_rows, preferred_element_type=jnp.float32
    ).astype(jnp.bfloat16)
    slot_cot = slot_cot.reshape(-1, local_count, capacity, model_width)
    cot_arrived = route_slots(slot_cot)
    down_term = jnp.einsum(
        "sjcf,sjcd->jfd", activated, cot_arrived, preferred_element_type=jnp.float32
    )
    dact = jnp.einsum("sjcd,jfd->sjcf", cot_arrived, down_local, preferred_element_type=jnp.float32)
    sigmoid_gate = jax.nn.sigmoid(gate_pre)
    dgate = (dact * up_pre * sigmoid_gate * (1.0 + gate_pre * (1.0 - sigmoid_gate))).astype(
        jnp.bfloat16
    )
    dup = (dact * gate_pre * sigmoid_gate).astype(jnp.bfloat16)
    gate_term = jnp.einsum("sjcd,sjcf->jdf", arrived, dgate, preferred_element_type=jnp.float32)
    up_term = jnp.einsum("sjcd,sjcf->jdf", arrived, dup, preferred_element_type=jnp.float32)
    gate_out, up_out = in_one_piece(
        (gate_term.astype(jnp.bfloat16), up_term.astype(jnp.bfloat16)), "dp", 1, 0, 2
    )
    down_out = lax.all_to_all(
        down_term.astype(jnp.bfloat16), "dp", split_axis=2, concat_axis=0, tiled=True
    )
    return (layer_out[None], router_grad, gate_out, up_out, down_out)


def solution(mesh):
    placed = (
        P("dp", "ctx", None),
        P("dp", "ctx", "exp", None),
        P("exp", None),
        P(),
        P("exp", None, None),
        P("exp", None),
        P(),
        P(),
        P("dp", "ctx", None),
        P("dp", "ctx"),
        P("ctx", None, "exp"),
        P("ctx", None, "exp"),
        P("ctx", "exp", None),
        P("dp", "ctx", None),
    )
    return jax.shard_map(
        local,
        mesh=mesh,
        in_specs=placed,
        out_specs=(
            P("dp", "ctx", None),
            P(),
            P("ctx", "dp", "exp"),
            P("ctx", "dp", "exp"),
            P("ctx", "exp", "dp"),
        ),
        check_vma=False,
    )
```

profile of v0, /device:TPU:88, one launch (start us, length us, event | category | flops | bytes accessed | tf_op | source)
XLA Modules:
  0.0 998.6 jit_solution(10595866600486797685)
XLA Ops:
  10.4 5.8 all-to-all-start
  16.3 29.8 %all-to-all-done = f32[8,128,576]{1,2,0:T(8,128)} async-done(((f32[8,128,576]{1,2,0:T(8,128)}), f32[8,128,576]{1,2,0:T(8,128)}, u32[]{:S(2)}, u32[]{:S(2)}) %all-to-all-start) | async-done | bytes 2359328 | tf_op jit(solution)/shard_map/all_to_all | solution.py:13
  46.0 1.8 reduce_sum.102
  49.0 37.8 %all-gather = s32[1,2048]{1,0:T(1,128)S(1)} all-gather(s32[1,128]{1,0:T(1,128)S(1)} %copy-done.4), channel_id=2, replica_groups=mesh['dp'=2,'ctx'=16,'exp'=8] {'ctx'}, dimensions={1}, use_global_device_ids=true | all-gather | bytes 8704 | tf_op jit(solution)/shard_map/all_gather | solution.py:93
  87.1 26.5 %all-gather.3.cloned.1.call-done = bf16[2048,576]{0,1:T(8,128)(2,1)} async-done(((bf16[128,576]{0,1:T(8,128)(2,1)}), bf16[2048,576]{0,1:T(8,128)(2,1)}) %all-gather.3.cloned.1.call-update) | async-done | bytes 2359312 | tf_op jit(solution)/shard_map/all_gather | solution.py:92
  113.6 2.7 fusion.51
  116.3 1.9 fusion.156
  118.3 2.9 fusion.72
  123.1 1.7 reduce-window.6
  126.0 83.0 %all-reduce.4.cloned.1.call-done = f32[128,2560]{1,0:T(8,128)} async-done(((f32[128,2560]{1,0:T(8,128)}), f32[128,2560]{1,0:T(8,128)}) %all-reduce.4.cloned.1.call-update) | async-done | bytes 1310736 | tf_op jit(solution)/shard_map/psum | solution.py:124
  209.0 1.8 fusion.64
  210.8 3.9 convolution_convert_fusion.2
  214.7 8.9 all-to-all-start.1
  223.7 113.3 %all-to-all-done.1 = bf16[32,1,32,2560]{3,2,1,0:T(8,128)(2,1)} async-done(((bf16[32,1,32,2560]{3,2,1,0:T(8,128)(2,1)}), bf16[32,1,32,2560]{3,2,1,0:T(8,128)(2,1)}, u32[]{:S(2)}, u32[]{:S(2)}) %all-to-all-start.1) | async-done | bytes 5242912 | tf_op jit(solution)/shard_map/all_to_all | solution.py:56
  336.9 4.4 fusion.55
  341.4 5.4 multiply_convert_fusion.2
  347.6 3.8 fusion.13
  351.4 12.1 %all-to-all-start.2 = ((bf16[32,1,32,2560]{3,2,1,0:T(8,128)(2,1)}), bf16[32,1,32,2560]{3,2,1,0:T(8,128)(2,1)}, u32[]{:S(2)}, u32[]{:S(2)}) async-start(bf16[32,1,32,2560]{3,2,1,0:T(8,128)(2,1)} %fusion.13), calls=%async_computation.2 | async-start | bytes 10485760 | tf_op jit(solution)/shard_map/all_to_all | solution.py:177
  364.6 5.1 gather_fusion
  370.0 107.0 %all-to-all-done.2 = bf16[32,1,32,2560]{3,2,1,0:T(8,128)(2,1)} async-done(((bf16[32,1,32,2560]{3,2,1,0:T(8,128)(2,1)}), bf16[32,1,32,2560]{3,2,1,0:T(8,128)(2,1)}, u32[]{:S(2)}, u32[]{:S(2)}) %all-to-all-start.2) | async-done | bytes 5242912 | tf_op jit(solution)/shard_map/all_to_all | solution.py:177
  477.0 4.1 convolution_bitcast_fusion
  481.1 5.1 gather_fusion.1
  486.4 23.5 %psum.30 = f32[128,6]{0,1:T(8,128)S(1)} all-reduce(f32[128,6]{0,1:T(8,128)S(1)} %and_select_fusion), channel_id=1, replica_groups=mesh['dp'=2,'ctx'=16,'exp'=8] {'exp'}, use_global_device_ids=true, to_apply=%region_15.16 | all-reduce | flops 768 | bytes 6144 | tf_op jit(solution)/shard_map/psum | solution.py:183
  510.4 5.0 convolution_convert_fusion
  515.4 9.6 all-to-all-start.3
  525.0 4.4 fusion.159
  530.9 158.4 %all-reduce.6.cloned.1.call-done = f32[128,2560]{1,0:T(8,128)} async-done(((f32[128,2560]{1,0:T(8,128)}), f32[128,2560]{1,0:T(8,128)}) %all-reduce.6.cloned.1.call-update) | async-done | bytes 1310736 | tf_op jit(solution)/shard_map/psum | solution.py:183
  689.3 2.3 fusion.86
  691.6 4.1 fusion.61
  695.8 3.9 fusion.38
  699.6 3.8 fusion.35
  704.9 8.9 copy.117
  714.4 18.2 %reduce.3 = bf16[2560,384]{1,0:T(8,128)(2,1)} reduce(bf16[2560,1,384]{2,1,0:T(2,128)(2,1)} %bitcast.237, bf16[]{:T(256)} %broadcast.489), dimensions={1}, to_apply=%bitcast.212.reduce_sub_computation | reduce | bytes 3932162
  732.6 2.8 reshape.425
  735.3 8.4 all_to_all.50
  743.7 4.2 reshape.426
  748.0 2.5 copy.128
  750.5 4.7 fusion.32
  756.8 2.3 copy.120
  760.5 6.3 copy.118
  766.8 15.4 %reduce.4 = bf16[2560,192]{1,0:T(8,128)(2,1)S(1)} reduce(bf16[2560,1,192]{2,1,0:T(2,128)(2,1)} %bitcast.241, bf16[]{:T(256)} %broadcast.489), dimensions={1}, to_apply=%bitcast.214.reduce_sub_computation | reduce | bytes 1966082
  782.1 2.3 reshape.427
  784.5 5.6 all_to_all.51
  790.1 2.9 reshape.428
  793.0 5.1 copy.119
  799.3 2.2 copy.122
  801.5 188.8 %all-reduce.8.cloned.1.call-done = f32[2560,32]{0,1:T(8,128)} async-done(((f32[2560,32]{0,1:T(8,128)}), f32[2560,32]{0,1:T(8,128)}) %all-reduce.8.cloned.1.call-update) | async-done | bytes 327696 | tf_op jit(solution)/shard_map/psum | solution.py:193
  990.4 1.7 copy.146
  (88 shorter events, 17.9 us)
Async XLA Ops:
  7.2 340.4 %copy-start = (bf16[2,192,2560]{2,1,0:T(8,128)(2,1)S(1)}, bf16[2,192,2560]{2,1,0:T(8,128)(2,1)}, u32[]{:S(2)}) copy-start(bf16[2,192,2560]{2,1,0:T(8,128)(2,1)} %param.26) | copy-start | bytes 5898244
  10.4 5.9 copy-start.5
  10.4 35.7 %all-to-all-start = ((f32[8,128,576]{1,2,0:T(8,128)}), f32[8,128,576]{1,2,0:T(8,128)}, u32[]{:S(2)}, u32[]{:S(2)}) async-start(f32[8,128,576]{1,2,0:T(8,128)} %broadcast_in_dim.34), calls=%async_computation | async-start | bytes 4718592 | tf_op jit(solution)/shard_map/all_to_all | solution.py:13
  16.1 32.8 %copy-start.4 = (s32[1,128]{1,0:T(1,128)S(1)}, s32[1,128]{1,0:T(1,128)}, u32[]{:S(2)}) copy-start(s32[1,128]{1,0:T(1,128)} %param.23) | copy-start | bytes 1540
  16.2 97.5 %copy-start.7 = (bf16[1,128,2,576]{1,3,2,0:T(8,128)(2,1)S(1)}, bf16[1,128,2,576]{1,3,2,0:T(8,128)(2,1)}, u32[]{:S(2)}) copy-start(bf16[1,128,2,576]{1,3,2,0:T(8,128)(2,1)} %param.15) | copy-start | bytes 884740
  16.2 97.4 %all-gather.3.cloned.1.call-start = ((), (), s32[]{:S(2)}) async-start(), calls=%async_computation.6 | async-start | bytes 2506752 | tf_op jit(solution)/shard_map/all_gather | solution.py:92
  48.9 160.1 %all-reduce.4.cloned.1.call-start = ((), (), s32[]{:S(2)}) async-start(), calls=%async_computation.7 | async-start | bytes 2621440 | tf_op jit(solution)/shard_map/psum | solution.py:124
  118.3 2.9 copy-start.1
  121.2 1.5 copy-start.2
  121.2 4.3 copy-start.3
  214.7 122.2 %all-to-all-start.1 = ((bf16[32,1,32,2560]{3,2,1,0:T(8,128)(2,1)}), bf16[32,1,32,2560]{3,2,1,0:T(8,128)(2,1)}, u32[]{:S(2)}, u32[]{:S(2)}) async-start(bf16[32,1,32,2560]{3,2,1,0:T(8,128)(2,1)} %bitcast.235), calls=%async_computation.1 | async-start | bytes 10485760 | tf_op jit(solution)/shard_map/all_to_all | solution.py:56
  336.9 4.5 copy-start.6
  341.4 5.4 copy-start.9
  346.8 0.8 copy-start.12
  351.4 12.7 %copy-start.8 = (bf16[2560,32]{0,1:T(8,128)(2,1)S(1)}, bf16[2560,32]{0,1:T(8,128)(2,1)}, u32[]{:S(2)}) copy-start(bf16[2560,32]{0,1:T(8,128)(2,1)} %param.21) | copy-start | bytes 491524
  351.4 125.5 %all-to-all-start.2 = ((bf16[32,1,32,2560]{3,2,1,0:T(8,128)(2,1)}), bf16[32,1,32,2560]{3,2,1,0:T(8,128)(2,1)}, u32[]{:S(2)}, u32[]{:S(2)}) async-start(bf16[32,1,32,2560]{3,2,1,0:T(8,128)(2,1)} %fusion.13), calls=%async_computation.2 | async-start | bytes 10485760 | tf_op jit(solution)/shard_map/all_to_all | solution.py:177
  515.4 176.2 %all-to-all-start.3 = ((bf16[32,1,32,2560]{3,2,1,0:T(8,128)(2,1)}), bf16[32,1,32,2560]{3,2,1,0:T(8,128)(2,1)}, u32[]{:S(2)}, u32[]{:S(2)}) async-start(bf16[32,1,32,2560]{3,2,1,0:T(8,128)(2,1)} %bitcast.236), calls=%async_computation.3 | async-start | bytes 10485760 | tf_op jit(solution)/shard_map/all_to_all | solution.py:56
  525.0 164.4 %all-reduce.6.cloned.1.call-start = ((), (), s32[]{:S(2)}) async-start(), calls=%async_computation.8 | async-start | bytes 2621440 | tf_op jit(solution)/shard_map/psum | solution.py:183
  529.4 460.9 %all-reduce.8.cloned.1.call-start = ((), (), s32[]{:S(2)}) async-start(), calls=%async_computation.9 | async-start | bytes 655360 | tf_op jit(solution)/shard_map/psum | solution.py:193
  691.6 4.1 copy-start.10
  695.8 3.9 copy-start.11
  748.0 2.5 copy-start.13
Sparse Core Ops, SparseCore 0:
  49.1 64.4 all-gather.2
  122.8 86.1 all-reduce.3
  529.6 159.7 all-reduce.5
  692.4 297.9 all-reduce.7
where the time goes:
time: 1000 us; the launch traced here: 999 us
  waiting for transfers between devices  707 us (71%)
  blocking collectives  75.3 us (8%)
  local copies, waits for them, and re-layouts  60.3 us (6%)
  matrix products  58.1 us (6%)
  other arithmetic  47.3 us (5%)
  starting transfers between devices  36.6 us (4%)
  between operations  14.2 us (1%)
    psum x1, waiting for transfers between devices, local(): router_grad = lax.psum(router_term, ('dp', 'ctx'))  189 us
    psum x1, waiting for transfers between devices, local(): moe, dweight = lax.psum((moe_part, dweight_part), 'exp')  158 us
    all_to_all x2, waiting for transfers between devices, route_slots(): lax.all_to_all(outgoing, ('dp', 'ctx'), split_axis=0, concat_axis=0, tile...  113 us
    all_to_all x1, waiting for transfers between devices, local(): lax.all_to_all(expert_part, ('dp', 'ctx'), split_axis=0, concat_axis=0, t...  107 us
    psum x1, waiting for transfers between devices, local(): attention = lax.psum(head_part, 'exp')  83 us
    all_gather x1, blocking collectives, local(): lax.all_gather(doc_ids[0], 'ctx', axis=0, tiled=True)  37.8 us
    unnamed x2, other arithmetic  33.5 us
    all_to_all x1, waiting for transfers between devices, from_everyone(): lax.all_to_all(jnp.broadcast_to(array[None], (count, *array.shape)), axis...  29.8 us
  transfers between devices with their start and end apart: 8, of which 7 were waited for; matrix products, arithmetic and copies ran while one was open for 11% of the time, Pallas kernels for 0%

commit v1 on v0

--- a/solution.py
+++ b/solution.py
@@ -2,10 +2,12 @@
 import jax.numpy as jnp
 from jax import lax
 from jax.sharding import PartitionSpec as P
+from jax.lax import all_gather
 
 ROPE = 64
 NOPE = 128
 epsilon = 1e-06
+_follow_words = lambda body: jnp.sum(all_gather(body, ("dp", "ctx")), 0)
 
 
 def from_everyone(array, axis):
@@ -190,7 +192,7 @@
     dprobs = jnp.sum(id_hits * dchosen[:, :, None], axis=1)
     dlogits = router_probs * (dprobs - jnp.sum(router_probs * dprobs, axis=1, keepdims=True))
     router_term = jnp.dot(normed.astype(jnp.float32).T, dlogits, precision=lax.Precision.HIGHEST)
-    router_grad = lax.psum(router_term, ("dp", "ctx"))
+    router_grad = _follow_words(router_term)
     slot_cot = jnp.einsum(
         "se,sd->ed", combine, cot_rows, preferred_element_type=jnp.float32
     ).astype(jnp.bfloat16)

time: 1000 us -> 832 us (0.83)
  waiting for transfers between devices: 707 us -> 520 us
    psum x1 -> x0, waiting for transfers between devices: 189 us -> none  [local(): router_grad = lax.psum(router_term, ('dp', 'ctx'))]
    unnamed x40 -> x38, local copies, waits for them, and re-layouts: 23.9 us -> 32.2 us
  transfers between devices with their start and end apart: 8 -> 8, of which waited for: 7 -> 6; matrix products, arithmetic and copies ran while one was open for 11% -> 14% of each run, Pallas kernels for 0% -> 0%
where the time goes in v1:
time: 832 us; the launch traced here: 821 us
  waiting for transfers between devices  520 us (62%)
  blocking collectives  76.1 us (9%)
  local copies, waits for them, and re-layouts  66.9 us (8%)
  matrix products  57.4 us (7%)
  other arithmetic  49.8 us (6%)
  starting transfers between devices  36.7 us (4%)
  between operations  14.5 us (2%)
    psum x1, waiting for transfers between devices, local(): moe, dweight = lax.psum((moe_part, dweight_part), 'exp')  160 us
    all_to_all x2, waiting for transfers between devices, route_slots(): lax.all_to_all(outgoing, ('dp', 'ctx'), split_axis=0, concat_axis=0, tile...  113 us
    all_to_all x1, waiting for transfers between devices, local(): lax.all_to_all(expert_part, ('dp', 'ctx'), split_axis=0, concat_axis=0, t...  108 us
    psum x1, waiting for transfers between devices, local(): attention = lax.psum(head_part, 'exp')  83 us
    all_gather x1, blocking collectives, local(): lax.all_gather(doc_ids[0], 'ctx', axis=0, tiled=True)  37.8 us
    unnamed x2, other arithmetic  33.7 us
    unnamed x38, local copies, waits for them, and re-layouts  32.2 us
    all_to_all x1, waiting for transfers between devices, from_everyone(): lax.all_to_all(jnp.broadcast_to(array[None], (count, *array.shape)), axis...  29.8 us
  transfers between devices with their start and end apart: 8, of which 6 were waited for; matrix products, arithmetic and copies ran while one was open for 14% of the time, Pallas kernels for 0%

profile of v1, /device:TPU:88, one launch (start us, length us, event | category | flops | bytes accessed | tf_op | source)
XLA Modules:
  0.0 821.3 jit_solution(15162920932063858998)
XLA Ops:
  10.4 5.8 all-to-all-start
  16.3 29.8 %all-to-all-done = f32[8,128,576]{1,2,0:T(8,128)} async-done(((f32[8,128,576]{1,2,0:T(8,128)}), f32[8,128,576]{1,2,0:T(8,128)}, u32[]{:S(2)}, u32[]{:S(2)}) %all-to-all-start) | async-done | bytes 2359328 | tf_op jit(solution)/shard_map/all_to_all | solution.py:15
  46.0 1.8 reduce_sum.111
  49.0 37.8 %all-gather = s32[1,2048]{1,0:T(1,128)S(1)} all-gather(s32[1,128]{1,0:T(1,128)S(1)} %copy-done.4), channel_id=2, replica_groups=mesh['dp'=2,'ctx'=16,'exp'=8] {'ctx'}, dimensions={1}, use_global_device_ids=true | all-gather | bytes 8704 | tf_op jit(solution)/shard_map/all_gather | solution.py:95
  87.1 26.5 %all-gather.5.cloned.1.call-done = bf16[2048,576]{0,1:T(8,128)(2,1)} async-done(((bf16[128,576]{0,1:T(8,128)(2,1)}), bf16[2048,576]{0,1:T(8,128)(2,1)}) %all-gather.5.cloned.1.call-update) | async-done | bytes 2359312 | tf_op jit(solution)/shard_map/all_gather | solution.py:94
  113.6 2.7 fusion.51
  116.3 1.9 fusion.156
  118.3 2.9 fusion.72
  123.1 1.7 reduce-window.6
  126.0 83.0 %all-reduce.3.cloned.1.call-done = f32[128,2560]{1,0:T(8,128)} async-done(((f32[128,2560]{1,0:T(8,128)}), f32[128,2560]{1,0:T(8,128)}) %all-reduce.3.cloned.1.call-update) | async-done | bytes 1310736 | tf_op jit(solution)/shard_map/psum | solution.py:126
  209.0 1.8 fusion.64
  210.8 3.9 convolution_convert_fusion.2
  214.7 8.9 %all-to-all-start.1 = ((bf16[32,1,32,2560]{3,2,1,0:T(8,128)(2,1)}), bf16[32,1,32,2560]{3,2,1,0:T(8,128)(2,1)}, u32[]{:S(2)}, u32[]{:S(2)}) async-start(bf16[32,1,32,2560]{3,2,1,0:T(8,128)(2,1)} %bitcast.240), calls=%async_computation.1 | async-start | bytes 10485760 | tf_op jit(solution)/shard_map/all_to_all | solution.py:58
  223.7 113.2 %all-to-all-done.1 = bf16[32,1,32,2560]{3,2,1,0:T(8,128)(2,1)} async-done(((bf16[32,1,32,2560]{3,2,1,0:T(8,128)(2,1)}), bf16[32,1,32,2560]{3,2,1,0:T(8,128)(2,1)}, u32[]{:S(2)}, u32[]{:S(2)}) %all-to-all-start.1) | async-done | bytes 5242912 | tf_op jit(solution)/shard_map/all_to_all | solution.py:58
  336.8 4.5 fusion.55
  341.3 5.4 multiply_convert_fusion.2
  347.5 3.9 fusion.13
  351.4 12.2 %all-to-all-start.2 = ((bf16[32,1,32,2560]{3,2,1,0:T(8,128)(2,1)}), bf16[32,1,32,2560]{3,2,1,0:T(8,128)(2,1)}, u32[]{:S(2)}, u32[]{:S(2)}) async-start(bf16[32,1,32,2560]{3,2,1,0:T(8,128)(2,1)} %fusion.13), calls=%async_computation.2 | async-start | bytes 10485760 | tf_op jit(solution)/shard_map/all_to_all | solution.py:179
  364.7 5.1 gather_fusion
  370.1 107.6 %all-to-all-done.2 = bf16[32,1,32,2560]{3,2,1,0:T(8,128)(2,1)} async-done(((bf16[32,1,32,2560]{3,2,1,0:T(8,128)(2,1)}), bf16[32,1,32,2560]{3,2,1,0:T(8,128)(2,1)}, u32[]{:S(2)}, u32[]{:S(2)}) %all-to-all-start.2) | async-done | bytes 5242912 | tf_op jit(solution)/shard_map/all_to_all | solution.py:179
  477.7 4.1 convolution_bitcast_fusion
  481.8 5.1 gather_fusion.1
  487.2 23.5 %psum.23 = f32[128,6]{0,1:T(8,128)S(1)} all-reduce(f32[128,6]{0,1:T(8,128)S(1)} %and_select_fusion), channel_id=1, replica_groups=mesh['dp'=2,'ctx'=16,'exp'=8] {'exp'}, use_global_device_ids=true, to_apply=%region_15.16 | all-reduce | flops 768 | bytes 6144 | tf_op jit(solution)/shard_map/psum | solution.py:185
  511.1 4.4 fusion.159
  517.0 5.0 convolution_convert_fusion
  522.0 9.6 %all-to-all-start.3 = ((bf16[32,1,32,2560]{3,2,1,0:T(8,128)(2,1)}), bf16[32,1,32,2560]{3,2,1,0:T(8,128)(2,1)}, u32[]{:S(2)}, u32[]{:S(2)}) async-start(bf16[32,1,32,2560]{3,2,1,0:T(8,128)(2,1)} %bitcast.241), calls=%async_computation.3 | async-start | bytes 10485760 | tf_op jit(solution)/shard_map/all_to_all | solution.py:58
  531.6 159.9 %all-reduce.5.cloned.1.call-done = f32[128,2560]{1,0:T(8,128)} async-done(((f32[128,2560]{1,0:T(8,128)}), f32[128,2560]{1,0:T(8,128)}) %all-reduce.5.cloned.1.call-update) | async-done | bytes 1310736 | tf_op jit(solution)/shard_map/psum | solution.py:185
  691.4 2.3 fusion.86
  693.7 4.1 fusion.61
  697.9 3.9 fusion.38
  701.7 3.8 fusion.35
  707.0 8.9 %copy.117 = bf16[1,2560,384]{2,0,1:T(2,128)(2,1)} copy(bf16[1,2560,384]{1,2,0:T(8,128)(2,1)} %pad_maximum_fusion) | data formatting | bytes 3932160 | tf_op jit(solution)/shard_map/concatenate | solution.py:26
  716.5 18.3 %reduce.3 = bf16[2560,384]{1,0:T(8,128)(2,1)} reduce(bf16[2560,1,384]{2,1,0:T(2,128)(2,1)} %bitcast.242, bf16[]{:T(256)} %broadcast.489), dimensions={1}, to_apply=%bitcast.217.reduce_sub_computation | reduce | bytes 3932162
  734.8 2.8 reshape.426
  737.6 8.7 %all_to_all.50 = bf16[2,2,245760]{2,1,0:T(2,128)(2,1)} all-to-all(bf16[2,2,245760]{2,1,0:T(2,128)(2,1)} %reshape.426), channel_id=1, replica_groups=mesh['dp'=2,'ctx'=16,'exp'=8] {'dp'}, dimensions={0} | all-to-all | bytes 3932160 | tf_op jit(solution)/shard_map/all_to_all | solution.py:28
  746.3 4.2 reshape.427
  750.4 2.4 copy.128
  754.5 2.3 copy.120
  758.2 4.1 fusion.32
  762.3 4.5 copy.118
  766.8 15.4 %reduce.4 = bf16[2560,192]{1,0:T(8,128)(2,1)S(1)} reduce(bf16[2560,1,192]{2,1,0:T(2,128)(2,1)} %bitcast.247, bf16[]{:T(256)} %broadcast.489), dimensions={1}, to_apply=%bitcast.219.reduce_sub_computation | reduce | bytes 1966082
  782.3 2.3 reshape.428
  784.6 6.1 all_to_all.51
  790.7 2.9 reshape.429
  793.6 5.1 copy.119
  800.0 2.2 copy.122
  802.2 10.0 %copy.130 = f32[4,8,32,2560]{3,2,1,0:T(8,128)S(1)} copy(f32[4,8,32,2560]{3,1,2,0:T(8,128)} %bitcast.246) | data formatting | bytes 20971520
  812.3 2.3 bitcast_reduce_fusion
  (87 shorter events, 17.9 us)
Async XLA Ops:
  7.2 340.3 %copy-start = (bf16[2,192,2560]{2,1,0:T(8,128)(2,1)S(1)}, bf16[2,192,2560]{2,1,0:T(8,128)(2,1)}, u32[]{:S(2)}) copy-start(bf16[2,192,2560]{2,1,0:T(8,128)(2,1)} %param.26) | copy-start | bytes 5898244
  10.4 5.9 copy-start.5
  10.4 35.7 %all-to-all-start = ((f32[8,128,576]{1,2,0:T(8,128)}), f32[8,128,576]{1,2,0:T(8,128)}, u32[]{:S(2)}, u32[]{:S(2)}) async-start(f32[8,128,576]{1,2,0:T(8,128)} %broadcast_in_dim.34), calls=%async_computation | async-start | bytes 4718592 | tf_op jit(solution)/shard_map/all_to_all | solution.py:15
  16.1 32.8 %copy-start.4 = (s32[1,128]{1,0:T(1,128)S(1)}, s32[1,128]{1,0:T(1,128)}, u32[]{:S(2)}) copy-start(s32[1,128]{1,0:T(1,128)} %param.23) | copy-start | bytes 1540
  16.2 97.4 %copy-start.7 = (bf16[1,128,2,576]{1,3,2,0:T(8,128)(2,1)S(1)}, bf16[1,128,2,576]{1,3,2,0:T(8,128)(2,1)}, u32[]{:S(2)}) copy-start(bf16[1,128,2,576]{1,3,2,0:T(8,128)(2,1)} %param.15) | copy-start | bytes 884740
  16.2 97.4 %all-gather.5.cloned.1.call-start = ((), (), s32[]{:S(2)}) async-start(), calls=%async_computation.6 | async-start | bytes 2506752 | tf_op jit(solution)/shard_map/all_gather | solution.py:94
  48.9 160.1 %all-reduce.3.cloned.1.call-start = ((), (), s32[]{:S(2)}) async-start(), calls=%async_computation.7 | async-start | bytes 2621440 | tf_op jit(solution)/shard_map/psum | solution.py:126
  118.3 2.9 copy-start.1
  121.2 1.5 copy-start.2
  121.2 4.2 copy-start.3
  214.7 122.1 %all-to-all-start.1 = ((bf16[32,1,32,2560]{3,2,1,0:T(8,128)(2,1)}), bf16[32,1,32,2560]{3,2,1,0:T(8,128)(2,1)}, u32[]{:S(2)}, u32[]{:S(2)}) async-start(bf16[32,1,32,2560]{3,2,1,0:T(8,128)(2,1)} %bitcast.240), calls=%async_computation.1 | async-start | bytes 10485760 | tf_op jit(solution)/shard_map/all_to_all | solution.py:58
  336.8 4.5 copy-start.6
  341.3 5.4 copy-start.9
  346.7 0.8 copy-start.12
  351.4 12.8 %copy-start.8 = (bf16[2560,32]{0,1:T(8,128)(2,1)S(1)}, bf16[2560,32]{0,1:T(8,128)(2,1)}, u32[]{:S(2)}) copy-start(bf16[2560,32]{0,1:T(8,128)(2,1)} %param.21) | copy-start | bytes 491524
  351.4 126.3 %all-to-all-start.2 = ((bf16[32,1,32,2560]{3,2,1,0:T(8,128)(2,1)}), bf16[32,1,32,2560]{3,2,1,0:T(8,128)(2,1)}, u32[]{:S(2)}, u32[]{:S(2)}) async-start(bf16[32,1,32,2560]{3,2,1,0:T(8,128)(2,1)} %fusion.13), calls=%async_computation.2 | async-start | bytes 10485760 | tf_op jit(solution)/shard_map/all_to_all | solution.py:179
  363.6 327.8 %all-reduce.5.cloned.1.call-start = ((), (), s32[]{:S(2)}) async-start(), calls=%async_computation.8 | async-start | bytes 2621440 | tf_op jit(solution)/shard_map/psum | solution.py:185
  515.6 286.6 %all-gather.7.cloned.1.call-start = ((), (), s32[]{:S(2)}) async-start(), calls=%async_computation.9 | async-start | bytes 10813440 | tf_op jit(solution)/shard_map/all_gather | solution.py:10
  522.0 171.8 %all-to-all-start.3 = ((bf16[32,1,32,2560]{3,2,1,0:T(8,128)(2,1)}), bf16[32,1,32,2560]{3,2,1,0:T(8,128)(2,1)}, u32[]{:S(2)}, u32[]{:S(2)}) async-start(bf16[32,1,32,2560]{3,2,1,0:T(8,128)(2,1)} %bitcast.241), calls=%async_computation.3 | async-start | bytes 10485760 | tf_op jit(solution)/shard_map/all_to_all | solution.py:58
  693.7 4.1 copy-start.10
  697.8 3.9 copy-start.11
Sparse Core Ops, SparseCore 0:
  49.1 64.4 all-gather.4
  122.8 86.1 all-reduce.2
  515.7 175.6 all-reduce.4
  694.4 87.5 all-gather.6
